TPU v7x, 32 devices: a whole 2x2x4 slice. The times are simulated.
32 devices in a mesh: grp: 2 (over x), chan: 16 (over z, y, core).
Axes of the slice: x: 2, y: 2, z: 4, core: 2. Of those that a mesh axis runs over, the one named last changes fastest.
Arguments:
- samples: bfloat16 [32, 16, 256, 1024], P(('grp', 'chan')), parts along dimension 0, may hold values from -6 to 6
- fir: float32 [16, 1024], replicated, may hold values from -1.5 to 1.5
- chan_assign: int32 [256], replicated, may hold values from 0 to 511, as said below
- input_order: int32 [1024], replicated, may hold values from 0 to 1023, each once
Outputs:
- vis: bfloat16 [512, 1024, 1024], P(('grp', 'chan')), parts along dimension 0
There are 2 independent parts, one for each index of `grp`. A program takes and returns all parts, laid end to end along the dimension named above; an argument that names none is the same for every part. Nothing has to cross between parts.
Inputs may be any that keep to these rules, and one draw needn't show every extreme that they name: `chan_assign`: distinct transform bins; bin 0 and bin 1024 // 2 - 1 are always among them. `input_order`: each input number once.
All inputs are finite; a program needn't handle non-finite values.
Results may differ from a plain program's by a relative error of at most 0.0074.
Values may be sent and summed in bfloat16 or wider, within the bound.
No kernel may reach another device: no remote copies, remote signals or barrier semaphores. Data moves between devices by JAX's collectives and lax.ppermute only.
A program may use at most 256 MiB of HBM per device.

v0:
```python
import math
import jax
import jax.numpy as jnp
from jax import lax
from jax.sharding import PartitionSpec as P

QUART = 4


def shifted(value, axis, steps):
    count = lax.axis_size(axis)
    initial, last = (max(0, -steps), min(count, count - steps))
    return lax.ppermute(value, axis, [(source, source + steps) for source in range(initial, last)])


def make_table(chan_assign, frame_len):
    samples_index = jnp.arange(frame_len, dtype=jnp.int32)
    phase_index = chan_assign[:, None] * samples_index[None, :] % frame_len
    angles = phase_index.astype(jnp.float32) * (2.0 * math.pi / frame_len)
    norm_scale = 1.0 / math.sqrt(frame_len)
    return jnp.stack([jnp.cos(angles) * norm_scale, -jnp.sin(angles) * norm_scale]).astype(
        jnp.bfloat16
    )


def on_device(samples, fir, chan_assign, input_order):
    own_frames = samples[0]
    frames_quarter, slots_dev, frame_len = own_frames.shape
    taps_count = fir.shape[0]
    chan_count = lax.axis_size("chan")
    group_count = chan_count // QUART
    history_len = taps_count - 1
    lead_len = min(frames_quarter, history_len)
    tail_frames = own_frames[frames_quarter - lead_len :]
    pieces = shifted(tail_frames, "chan", 1 * group_count)
    extended = jnp.concatenate([pieces, own_frames], axis=0)
    dft_table = make_table(chan_assign, frame_len)
    chan_total = chan_assign.shape[0]
    chan_dev = chan_total // chan_count
    inputs_all = input_order.shape[0]
    inverse = jnp.argsort(input_order)
    spectra_total = QUART * frames_quarter
    accum = jnp.zeros((frames_quarter, slots_dev, frame_len), jnp.float32)
    for tap_index in range(taps_count):
        begin = 0 + history_len - tap_index
        accum = accum + fir[tap_index][None, None, :] * extended[
            begin : begin + frames_quarter
        ].astype(jnp.float32)
    filtered = accum.astype(jnp.bfloat16)
    spectra = jnp.einsum("pcn,fin->cfpi", dft_table, filtered, preferred_element_type=jnp.float32)
    spectra = spectra.astype(jnp.bfloat16).reshape(
        chan_count, chan_dev, frames_quarter, 2, slots_dev
    )
    received = lax.all_to_all(spectra, "chan", split_axis=0, concat_axis=4, tiled=True)
    items = received.shape[1]
    row_count = received.shape[2]
    split_parts = received.reshape(items, row_count, 2, QUART, inputs_all)
    ordered = jnp.take(split_parts, inverse, axis=4)
    stacked = ordered.reshape(items, row_count * 2 * QUART, inputs_all)
    real_rows = ordered[:, :, 0].reshape(items, row_count * QUART, inputs_all)
    imag_rows = ordered[:, :, 1].reshape(items, row_count * QUART, inputs_all)
    auto_sum = jnp.einsum("kra,krb->kab", stacked, stacked, preferred_element_type=jnp.float32)
    cross_sum = jnp.einsum("kra,krb->kab", real_rows, imag_rows, preferred_element_type=jnp.float32)
    row_index = lax.broadcasted_iota(jnp.int32, (inputs_all, inputs_all), 0)
    col_index = lax.broadcasted_iota(jnp.int32, (inputs_all, inputs_all), 1)
    upper_mask = (row_index <= col_index)[None, :, :]
    packed = (
        jnp.where(upper_mask, auto_sum, cross_sum - jnp.swapaxes(cross_sum, 1, 2)) / spectra_total
    )
    return packed.astype(jnp.bfloat16)


def solution(mesh):
    in_specs = (P(("grp", "chan"), None, None, None), P(), P(), P())
    out_specs = P(("grp", "chan"), None, None)
    return jax.shard_map(
        on_device, mesh=mesh, in_specs=in_specs, out_specs=out_specs, check_vma=False
    )
```

profile of v0, /device:TPU:13, one launch (start us, length us, event | category | flops | bytes accessed | tf_op | source)
XLA Modules:
  0.0 708.8 jit_solution(15074221744417982181)
XLA Ops:
  0.0 4.2 slice_bitcast_fusion
  4.2 3.2 collective-permute-start
  7.4 1.3 fusion.34
  8.7 5.6 multiply_convert_fusion.1
  14.3 161.9 %collective-permute-done = bf16[15,256,1024]{2,1,0:T(8,128)(2,1)} collective-permute-done((bf16[15,256,1024]{2,1,0:T(8,128)(2,1)S(1)}, bf16[15,256,1024]{2,1,0:T(8,128)(2,1)}, u32[]{:S(2)}, u32[]{:S(2)}) %collective-permute-start) | collective-permute-done | bytes 7864352 | tf_op jit(solution)/shard_map/ppermute | solution.py:13
  176.3 58.6 %fusion.41 = bf16[16,256,1024,1]{2,1,3,0:T(8,128)(2,1)} fusion(bf16[16,256,1024]{2,1,0:T(8,128)(2,1)} %bitcast.64, bf16[15,256,1024]{2,1,0:T(8,128)(2,1)} %collective-permute-done, f32[1024]{0:T(1024)S(1)} %bitcast.80, f32[1024]{0:T(1024)S(1)} %bitcast.81, f32[1024]{0:T(1024)S(1)} %bitcast.67, f32[1024]{0:T(1024)S(1)} %bitcast.68, ...), kind=kLoop, calls=%fused_computation.51.clone.clone.clone.2 | loop fusion | flops 264241152 | bytes 24707072 | tf_op jit(solution)/shard_map/pcn,fin->cfpi/dot_general | solution.py:50
  234.9 8.2 %fusion.20 = bf16[16,256,2,256]{1,3,2,0:T(8,128)(2,1)S(1)} fusion(bf16[1,256,1024]{2,1,0:T(8,128)(2,1)S(1)} %get-tuple-element.26, bf16[1,256,1024]{2,1,0:T(8,128)(2,1)S(1)} %get-tuple-element.25, bf16[16,256,1024,1]{2,1,3,0:T(8,128)(2,1)} %fusion.41), kind=kOutput, calls=%fused_computation.56 | convolution fusion | flops 4299161600 | bytes 13631488 | tf_op jit(solution)/shard_map/pcn,fin->cfpi/dot_general | solution.py:50
  243.1 0.0 copy-start
  243.1 6.5 copy.16
  249.6 7.4 %all-to-all-start = ((bf16[16,16,16,2,256]{4,3,2,1,0:T(2,128)(2,1)}), bf16[16,16,16,2,256]{4,3,2,1,0:T(2,128)(2,1)}, u32[]{:S(2)}, u32[]{:S(2)}) async-start(bf16[16,16,16,2,256]{4,3,2,1,0:T(2,128)(2,1)} %copy.16), calls=%async_computation | async-start | bytes 8388608 | tf_op jit(solution)/shard_map/all_to_all | solution.py:54
  257.0 0.0 copy-done
  257.0 4.4 sort.17
  261.3 0.3 iota_compare_fusion
  261.7 87.7 %all-to-all-done = bf16[16,16,16,2,256]{4,3,2,1,0:T(2,128)(2,1)} async-done(((bf16[16,16,16,2,256]{4,3,2,1,0:T(2,128)(2,1)}), bf16[16,16,16,2,256]{4,3,2,1,0:T(2,128)(2,1)}, u32[]{:S(2)}, u32[]{:S(2)}) %all-to-all-start) | async-done | bytes 4194336 | tf_op jit(solution)/shard_map/all_to_all | solution.py:54
  349.4 32.4 %copy.26 = bf16[1,16,16,2,16,256]{2,1,5,4,3,0:T(8,128)(2,1)} copy(bf16[1,16,16,2,16,256]{5,3,2,1,4,0:T(2,128)(2,1)} %bitcast.24) | data formatting | bytes 8388608 | tf_op jit(solution)/shard_map/reshape | solution.py:57
  381.8 36.7 %gather_fusion = bf16[1024,16,16,2,4]{2,1,4,3,0:T(8,128)(2,1)} fusion(bf16[16,16,2,4,1024]{1,0,4,3,2:T(8,128)(2,1)} %bitcast.63, s32[1024]{0:T(1024)S(1)} %fusion.31), kind=kCustom, calls=%fused_computation | custom fusion | bytes 8392704 | tf_op jit(solution)/shard_map/jit(_take)/gather | solution.py:58
  418.4 35.7 %copy.19 = bf16[16,16,2,4,1024]{4,0,3,2,1:T(8,128)(2,1)} copy(bf16[16,16,2,4,1024]{1,0,3,2,4:T(8,128)(2,1)} %bitcast.62) | data formatting | bytes 8388608 | tf_op jit(solution)/shard_map/jit(_take)/gather | solution.py:58
  454.1 22.7 %broadcast_select_fusion = bf16[16,16,2,4,1024]{1,0,3,2,4:T(8,128)(2,1)} fusion(pred[1024]{0:T(1024)(128)(4,1)S(1)} %compare_and_fusion, bf16[1024,16,16,2,4]{2,1,4,3,0:T(8,128)(2,1)} %gather_fusion), kind=kLoop, calls=%fused_computation.33 | loop fusion | flops 2097152 | bytes 8389632 | tf_op jit(solution)/shard_map/jit(_take)/select_n | solution.py:58
  476.9 4.5 bitcast_select_fusion
  481.3 25.2 %fusion.33 = (bf16[16,16,1,4,1024]{1,0,3,2,4:T(8,128)(2,1)}, bf16[16,16,1,4,1024]{1,0,3,2,4:T(8,128)(2,1)}) fusion(bf16[16,16,2,4,1024]{1,0,3,2,4:T(8,128)(2,1)} %broadcast_select_fusion), kind=kLoop, calls=%fused_computation.75 | loop fusion | bytes 8388608 | tf_op jit(solution)/shard_map/slice | solution.py:61
  506.6 21.9 %copy.23 = bf16[16,16,1,4,1024]{4,3,1,0,2:T(4,128)(2,1)} copy(bf16[16,16,1,4,1024]{1,0,3,2,4:T(8,128)(2,1)} %get-tuple-element.7) | data formatting | bytes 4194304 | tf_op jit(solution)/shard_map/slice | solution.py:61
  528.5 2.5 reshape_squeeze.7
  531.0 21.9 %copy.22 = bf16[16,16,1,4,1024]{4,3,1,0,2:T(4,128)(2,1)} copy(bf16[16,16,1,4,1024]{1,0,3,2,4:T(8,128)(2,1)} %get-tuple-element.8) | data formatting | bytes 4194304 | tf_op jit(solution)/shard_map/slice | solution.py:60
  552.9 4.0 reshape_squeeze.6
  556.9 24.8 %fusion.35 = f32[16,1024,1024]{2,1,0:T(8,128)} fusion(bf16[16,64,1024]{2,1,0:T(8,128)(2,1)} %reshape_squeeze.6, bf16[16,64,1024]{2,1,0:T(8,128)(2,1)S(1)} %reshape_squeeze.7), kind=kOutput, calls=%fused_computation.77 | convolution fusion | flops 2147483648 | bytes 71303168 | tf_op jit(solution)/shard_map/kra,krb->kab/dot_general | solution.py:63
  581.7 62.8 %copy.24 = f32[16,1024,1024]{1,2,0:T(8,128)} copy(f32[16,1024,1024]{2,1,0:T(8,128)} %fusion.35) | data formatting | bytes 134217728 | tf_op jit(solution)/shard_map/kra,krb->kab/dot_general | solution.py:63
  644.5 64.2 %fusion.2 = bf16[16,1024,1024]{2,1,0:T(8,128)(2,1)} fusion(f32[16,1024,1024]{2,1,0:T(8,128)} %fusion.35, f32[16,1024,1024]{1,2,0:T(8,128)} %copy.24, pred[1024,1024]{1,0:T(8,128)(4,1)S(1)} %iota_compare_fusion, bf16[16,128,1024]{2,0,1:T(8,128)(2,1)} %bitcast_select_fusion), kind=kOutput, calls=%fused_computation.4 | convolution fusion | flops 4362076160 | bytes 173015040 | tf_op jit(solution)/shard_map/kra,krb->kab/dot_general | solution.py:62
  (3 shorter events, 0.0 us)
Async XLA Ops:
  4.2 172.1 %collective-permute-start = (bf16[15,256,1024]{2,1,0:T(8,128)(2,1)S(1)}, bf16[15,256,1024]{2,1,0:T(8,128)(2,1)}, u32[]{:S(2)}, u32[]{:S(2)}) collective-permute-start(bf16[15,256,1024]{2,1,0:T(8,128)(2,1)S(1)} %slice_bitcast_fusion), channel_id=1, source_target_pairs={{0,4},{1,5},{2,6},{3,7},{4,8},{5,9},{6,10},{7,11},{8,12},{9,13},{1... | collective-permute-start | bytes 23592968 | tf_op jit(solution)/shard_map/ppermute | solution.py:13
  243.1 13.9 %copy-start = (s32[1024]{0:T(1024)S(1)}, s32[1024]{0:T(1024)}, u32[]{:S(2)}) copy-start(s32[1024]{0:T(1024)} %param.7) | copy-start | bytes 12292
  249.6 99.8 %all-to-all-start = ((bf16[16,16,16,2,256]{4,3,2,1,0:T(2,128)(2,1)}), bf16[16,16,16,2,256]{4,3,2,1,0:T(2,128)(2,1)}, u32[]{:S(2)}, u32[]{:S(2)}) async-start(bf16[16,16,16,2,256]{4,3,2,1,0:T(2,128)(2,1)} %copy.16), calls=%async_computation | async-start | bytes 8388608 | tf_op jit(solution)/shard_map/all_to_all | solution.py:54
where the time goes:
time: 714 us; the launch traced here: 709 us
  local copies, waits for them, and re-layouts  255 us (36%)
  waiting for transfers between devices  250 us (35%)
  matrix products  97.2 us (14%)
  other arithmetic  96.2 us (13%)
  starting transfers between devices  10.6 us (1%)
    ppermute x1, waiting for transfers between devices, shifted(): lax.ppermute(value, axis, [(source, source + steps) for source in range(i...  162 us
    all_to_all x1, waiting for transfers between devices, on_device(): lax.all_to_all(spectra, 'chan', split_axis=0, concat_axis=4, tiled=True)  87.7 us
    gather x2, local copies, waits for them, and re-layouts, on_device(): ordered = jnp.take(split_parts, inverse, axis=4)  72.4 us
    dot_general x1, matrix products, on_device(): jnp.einsum('kra,krb->kab', stacked, stacked, preferred_element_type=jnp.f...  64.2 us
    dot_general x1, local copies, waits for them, and re-layouts, on_device(): jnp.einsum('kra,krb->kab', real_rows, imag_rows, preferred_element_type=j...  62.8 us
    dot_general x1, other arithmetic, on_device(): jnp.einsum('pcn,fin->cfpi', dft_table, filtered, preferred_element_type=j...  58.6 us
    slice x2, local copies, waits for them, and re-layouts, on_device(): imag_rows = ordered[:, :, 1].reshape(items, row_count * QUART, inputs_all)  47.1 us
    reshape x1, local copies, waits for them, and re-layouts, on_device(): split_parts = received.reshape(items, row_count, 2, QUART, inputs_all)  32.4 us
  transfers between devices with their start and end apart: 2, of which 2 were waited for; matrix products, arithmetic and copies ran while one was open for 2% of the time, Pallas kernels for 0%

commit v1 on v0

--- a/solution.py
+++ b/solution.py
@@ -51,7 +51,18 @@
     spectra = spectra.astype(jnp.bfloat16).reshape(
         chan_count, chan_dev, frames_quarter, 2, slots_dev
     )
-    received = lax.all_to_all(spectra, "chan", split_axis=0, concat_axis=4, tiled=True)
+    ways, here = (lax.axis_size("chan"), lax.axis_index("chan"))
+    width = spectra.shape[0] // ways
+    lengths = list(spectra.shape)
+    lengths[0] = width
+    height = lengths[4]
+    lengths[4] = height * ways
+    received = jnp.zeros(lengths, spectra.dtype)
+    for mask in range(ways):
+        part = lax.dynamic_slice_in_dim(spectra, (here ^ mask) * width, width, axis=0)
+        if mask:
+            part = lax.ppermute(part, "chan", [(d, d ^ mask) for d in range(ways)])
+        received = lax.dynamic_update_slice_in_dim(received, part, (here ^ mask) * height, axis=4)
     items = received.shape[1]
     row_count = received.shape[2]
     split_parts = received.reshape(items, row_count, 2, QUART, inputs_all)

time: 714 us -> 780 us (1.092)
  the two profiles are of different devices: /device:TPU:13 before, /device:TPU:0 now
where the time goes in v1:
time: 780 us; the launch traced here: 767 us
  local copies, waits for them, and re-layouts  342 us (44%)
  waiting for transfers between devices  199 us (26%)
  other arithmetic  97.4 us (12%)
  matrix products  97.2 us (12%)
  starting transfers between devices  30.5 us (4%)
    ppermute x1, waiting for transfers between devices, shifted(): lax.ppermute(value, axis, [(source, source + steps) for source in range(i...  154 us
    gather x2, local copies, waits for them, and re-layouts, on_device(): ordered = jnp.take(split_parts, inverse, axis=4)  72.4 us
    dot_general x1, matrix products, on_device(): jnp.einsum('kra,krb->kab', stacked, stacked, preferred_element_type=jnp.f...  64.2 us
    ppermute x15, local copies, waits for them, and re-layouts, on_device(): part = lax.ppermute(part, 'chan', [(d, d ^ mask) for d in range(ways)])  63.6 us
    dot_general x1, local copies, waits for them, and re-layouts, on_device(): jnp.einsum('kra,krb->kab', real_rows, imag_rows, preferred_element_type=j...  62.9 us
    dot_general x1, other arithmetic, on_device(): jnp.einsum('pcn,fin->cfpi', dft_table, filtered, preferred_element_type=j...  58.2 us
    slice x2, local copies, waits for them, and re-layouts, on_device(): imag_rows = ordered[:, :, 1].reshape(items, row_count * QUART, inputs_all)  47.1 us
    ppermute x15, waiting for transfers between devices, on_device(): part = lax.ppermute(part, 'chan', [(d, d ^ mask) for d in range(ways)])  45.6 us
  transfers between devices with their start and end apart: 16, of which 6 were waited for; matrix products, arithmetic and copies ran while one was open for 17% of the time, Pallas kernels for 0%

profile of v1, /device:TPU:0, one launch (start us, length us, event | category | flops | bytes accessed | tf_op | source)
XLA Modules:
  0.0 766.6 jit_solution(13134633790247263691)
XLA Ops:
  0.0 7.7 %slice_bitcast_fusion = bf16[15,256,1024]{2,1,0:T(8,128)(2,1)} fusion(bf16[1,16,256,1024]{3,2,1,0:T(8,128)(2,1)} %param.4), kind=kLoop, calls=%fused_computation.52 | loop fusion | bytes 15728640 | tf_op jit(solution)/shard_map/slice | solution.py:34
  7.7 8.0 %collective-permute-start = (bf16[15,256,1024]{2,1,0:T(8,128)(2,1)}, bf16[15,256,1024]{2,1,0:T(8,128)(2,1)}, u32[]{:S(2)}, u32[]{:S(2)}) collective-permute-start(bf16[15,256,1024]{2,1,0:T(8,128)(2,1)} %slice_bitcast_fusion), channel_id=1, source_target_pairs={{0,4},{1,5},{2,6},{3,7},{4,8},{5,9},{6,10},{7,11},{8,12},{9,13},{1... | collective-permute-start | bytes 23592968 | tf_op jit(solution)/shard_map/ppermute | solution.py:13
  15.7 5.0 sort.17
  22.1 5.6 multiply_convert_fusion.1
  27.7 153.7 %collective-permute-done = bf16[15,256,1024]{2,1,0:T(8,128)(2,1)} collective-permute-done((bf16[15,256,1024]{2,1,0:T(8,128)(2,1)}, bf16[15,256,1024]{2,1,0:T(8,128)(2,1)}, u32[]{:S(2)}, u32[]{:S(2)}) %collective-permute-start) | collective-permute-done | bytes 7864352 | tf_op jit(solution)/shard_map/ppermute | solution.py:13
  181.5 58.2 %fusion.41 = bf16[16,256,1024,1]{2,1,3,0:T(8,128)(2,1)} fusion(bf16[16,256,1024]{2,1,0:T(8,128)(2,1)} %bitcast.61, bf16[15,256,1024]{2,1,0:T(8,128)(2,1)} %collective-permute-done, f32[1024]{0:T(1024)S(1)} %bitcast.77, f32[1024]{0:T(1024)S(1)} %bitcast.78, f32[1024]{0:T(1024)S(1)} %bitcast.64, f32[1024]{0:T(1024)S(1)} %bitcast.65, ...), kind=kLoop, calls=%fused_computation.51.clone.clone.clone.2 | loop fusion | flops 264241152 | bytes 24707072 | tf_op jit(solution)/shard_map/pcn,fin->cfpi/dot_general | solution.py:50
  239.7 8.2 %fusion.20 = bf16[16,256,2,256]{1,3,2,0:T(8,128)(2,1)S(1)} fusion(bf16[1,256,1024]{2,1,0:T(8,128)(2,1)S(1)} %get-tuple-element.42, bf16[1,256,1024]{2,1,0:T(8,128)(2,1)S(1)} %get-tuple-element.41, bf16[16,256,1024,1]{2,1,3,0:T(8,128)(2,1)} %fusion.41), kind=kOutput, calls=%fused_computation.56 | convolution fusion | flops 4299161600 | bytes 13631488 | tf_op jit(solution)/shard_map/pcn,fin->cfpi/dot_general | solution.py:50
  251.3 3.6 collective-permute-start.8
  258.0 3.5 collective-permute-start.6
  261.5 13.4 %collective-permute-done.2 = bf16[1,16,16,2,256]{4,1,0,3,2:T(8,128)(2,1)S(1)} collective-permute-done((bf16[1,16,16,2,256]{4,1,0,3,2:T(8,128)(2,1)S(1)}, bf16[1,16,16,2,256]{4,1,0,3,2:T(8,128)(2,1)S(1)}, u32[]{:S(2)}, u32[]{:S(2)}) %collective-permute-start.2) | collective-permute-done | bytes 262176 | tf_op jit(solution)/shard_map/ppermute | solution.py:64
  280.9 11.2 %broadcast_in_dim.32 = bf16[1,16,16,2,4096]{2,1,4,3,0:T(8,128)(2,1)} broadcast(bf16[]{:T(256)} %constant.17.clone.1), dimensions={} | broadcast | bytes 4194306 | tf_op jit(solution)/shard_map/broadcast_in_dim | solution.py:60
  293.7 4.5 copy.9
  301.3 3.7 copy.11
  307.8 4.5 copy.12
  313.9 4.5 copy.13
  318.4 3.4 collective-permute-start.13
  321.8 4.5 copy.14
  326.7 4.5 copy.15
  331.2 4.5 copy.16
  335.6 3.3 constant_dynamic-update-slice_fusion.14
  338.9 3.3 constant_dynamic-update-slice_fusion.13
  342.2 22.9 %collective-permute-done.9 = bf16[1,16,16,2,256]{4,1,0,3,2:T(8,128)(2,1)} collective-permute-done((bf16[1,16,16,2,256]{4,1,0,3,2:T(8,128)(2,1)}, bf16[1,16,16,2,256]{4,1,0,3,2:T(8,128)(2,1)}, u32[]{:S(2)}, u32[]{:S(2)}) %collective-permute-start.9) | collective-permute-done | bytes 262176 | tf_op jit(solution)/shard_map/ppermute | solution.py:64
  365.8 4.5 copy.17
  372.0 3.4 constant_dynamic-update-slice_fusion.11
  375.4 5.6 collective-permute-done.10
  381.0 4.5 copy.18
  385.5 3.3 constant_dynamic-update-slice_fusion.10
  388.7 3.3 constant_dynamic-update-slice_fusion.9
  394.6 4.7 copy.19
  401.0 3.4 constant_dynamic-update-slice_fusion.7
  404.4 4.5 copy.20
  408.9 3.3 constant_dynamic-update-slice_fusion.6
  415.5 4.5 copy.21
  421.6 3.3 constant_dynamic-update-slice_fusion.3
  424.9 3.6 copy.22
  428.5 3.3 constant_dynamic-update-slice_fusion.2
  433.5 3.6 copy.23
  438.8 36.7 %gather_fusion = bf16[1024,16,16,2,4]{2,1,4,3,0:T(8,128)(2,1)} fusion(bf16[16,16,2,4,1024]{1,0,4,3,2:T(8,128)(2,1)} %bitcast.60, s32[1024]{0:T(1024)S(1)} %fusion.31), kind=kCustom, calls=%fused_computation | custom fusion | bytes 8392704 | tf_op jit(solution)/shard_map/jit(_take)/gather | solution.py:69
  475.5 35.7 %copy.24 = bf16[16,16,2,4,1024]{4,0,3,2,1:T(8,128)(2,1)} copy(bf16[16,16,2,4,1024]{1,0,3,2,4:T(8,128)(2,1)} %bitcast.59) | data formatting | bytes 8388608 | tf_op jit(solution)/shard_map/jit(_take)/gather | solution.py:69
  511.2 22.7 %broadcast_select_fusion = bf16[16,16,2,4,1024]{1,0,3,2,4:T(8,128)(2,1)} fusion(pred[1024]{0:T(1024)(128)(4,1)S(1)} %compare_and_fusion, bf16[1024,16,16,2,4]{2,1,4,3,0:T(8,128)(2,1)} %gather_fusion), kind=kLoop, calls=%fused_computation.33 | loop fusion | flops 2097152 | bytes 8389632 | tf_op jit(solution)/shard_map/jit(_take)/select_n | solution.py:69
  534.0 4.5 bitcast_select_fusion
  538.5 25.2 %fusion.33 = (bf16[16,16,1,4,1024]{1,0,3,2,4:T(8,128)(2,1)}, bf16[16,16,1,4,1024]{1,0,3,2,4:T(8,128)(2,1)}) fusion(bf16[16,16,2,4,1024]{1,0,3,2,4:T(8,128)(2,1)} %broadcast_select_fusion), kind=kLoop, calls=%fused_computation.107 | loop fusion | bytes 8388608 | tf_op jit(solution)/shard_map/slice | solution.py:72
  563.7 21.9 %copy.28 = bf16[16,16,1,4,1024]{4,3,1,0,2:T(4,128)(2,1)} copy(bf16[16,16,1,4,1024]{1,0,3,2,4:T(8,128)(2,1)} %get-tuple-element.7) | data formatting | bytes 4194304 | tf_op jit(solution)/shard_map/slice | solution.py:72
  588.4 21.9 %copy.27 = bf16[16,16,1,4,1024]{4,3,1,0,2:T(4,128)(2,1)} copy(bf16[16,16,1,4,1024]{1,0,3,2,4:T(8,128)(2,1)} %get-tuple-element.8) | data formatting | bytes 4194304 | tf_op jit(solution)/shard_map/slice | solution.py:71
  610.3 4.0 reshape_squeeze.6
  614.2 24.8 %fusion.35 = f32[16,1024,1024]{2,1,0:T(8,128)} fusion(bf16[16,64,1024]{2,1,0:T(8,128)(2,1)} %reshape_squeeze.6, bf16[16,64,1024]{2,1,0:T(8,128)(2,1)S(1)} %reshape_squeeze.7), kind=kOutput, calls=%fused_computation.109 | convolution fusion | flops 2147483648 | bytes 71303168 | tf_op jit(solution)/shard_map/kra,krb->kab/dot_general | solution.py:74
  639.0 62.9 %copy.29 = f32[16,1024,1024]{1,2,0:T(8,128)} copy(f32[16,1024,1024]{2,1,0:T(8,128)} %fusion.35) | data formatting | bytes 134217728 | tf_op jit(solution)/shard_map/kra,krb->kab/dot_general | solution.py:74
  701.9 64.2 %fusion.2 = bf16[16,1024,1024]{2,1,0:T(8,128)(2,1)} fusion(f32[16,1024,1024]{2,1,0:T(8,128)} %fusion.35, f32[16,1024,1024]{1,2,0:T(8,128)} %copy.29, pred[1024,1024]{1,0:T(8,128)(4,1)S(1)} %copy-done, bf16[16,128,1024]{2,0,1:T(8,128)(2,1)} %bitcast_select_fusion), kind=kOutput, calls=%fused_computation.4 | convolution fusion | flops 4362076160 | bytes 173015040 | tf_op jit(solution)/shard_map/kra,krb->kab/dot_general | solution.py:73
  (56 shorter events, 41.3 us)
Async XLA Ops:
  7.7 173.7 %collective-permute-start = (bf16[15,256,1024]{2,1,0:T(8,128)(2,1)}, bf16[15,256,1024]{2,1,0:T(8,128)(2,1)}, u32[]{:S(2)}, u32[]{:S(2)}) collective-permute-start(bf16[15,256,1024]{2,1,0:T(8,128)(2,1)} %slice_bitcast_fusion), channel_id=1, source_target_pairs={{0,4},{1,5},{2,6},{3,7},{4,8},{5,9},{6,10},{7,11},{8,12},{9,13},{1... | collective-permute-start | bytes 23592968 | tf_op jit(solution)/shard_map/ppermute | solution.py:13
  249.5 8.5 %collective-permute-start.3 = (bf16[1,16,16,2,256]{4,1,0,3,2:T(8,128)(2,1)S(1)}, bf16[1,16,16,2,256]{4,1,0,3,2:T(8,128)(2,1)S(1)}, u32[]{:S(2)}, u32[]{:S(2)}) collective-permute-start(bf16[1,16,16,2,256]{4,1,0,3,2:T(8,128)(2,1)S(1)} %get-tuple-element.21), channel_id=1, source_target_pairs={{0,3},{1,2},{2,1},{3,0},{4,7},{5,6},{6,5},{7,4},{8,11},{9,10},{10,... | collective-permute-start | bytes 786440 | tf_op jit(solution)/shard_map/ppermute | solution.py:64
  249.6 25.4 %collective-permute-start.2 = (bf16[1,16,16,2,256]{4,1,0,3,2:T(8,128)(2,1)S(1)}, bf16[1,16,16,2,256]{4,1,0,3,2:T(8,128)(2,1)S(1)}, u32[]{:S(2)}, u32[]{:S(2)}) collective-permute-start(bf16[1,16,16,2,256]{4,1,0,3,2:T(8,128)(2,1)S(1)} %get-tuple-element.22), channel_id=1, source_target_pairs={{0,2},{1,3},{2,0},{3,1},{4,6},{5,7},{6,4},{7,5},{8,10},{9,11},{10,... | collective-permute-start | bytes 786440 | tf_op jit(solution)/shard_map/ppermute | solution.py:64
  251.0 26.1 %collective-permute-start.1 = (bf16[1,16,16,2,256]{4,1,0,3,2:T(8,128)(2,1)S(1)}, bf16[1,16,16,2,256]{4,1,0,3,2:T(8,128)(2,1)S(1)}, u32[]{:S(2)}, u32[]{:S(2)}) collective-permute-start(bf16[1,16,16,2,256]{4,1,0,3,2:T(8,128)(2,1)S(1)} %get-tuple-element.23), channel_id=1, source_target_pairs={{0,1},{1,0},{2,3},{3,2},{4,5},{5,4},{6,7},{7,6},{8,9},{9,8},{10,11... | collective-permute-start | bytes 786440 | tf_op jit(solution)/shard_map/ppermute | solution.py:64
  251.3 79.8 %collective-permute-start.8 = (bf16[1,16,16,2,256]{4,1,0,3,2:T(8,128)(2,1)}, bf16[1,16,16,2,256]{4,1,0,3,2:T(8,128)(2,1)}, u32[]{:S(2)}, u32[]{:S(2)}) collective-permute-start(bf16[1,16,16,2,256]{4,1,0,3,2:T(8,128)(2,1)} %get-tuple-element.16), channel_id=1, source_target_pairs={{0,8},{1,9},{2,10},{3,11},{4,12},{5,13},{6,14},{7,15},{8,0},{9,1},... | collective-permute-start | bytes 786440 | tf_op jit(solution)/shard_map/ppermute | solution.py:64
  254.9 71.4 %collective-permute-start.7 = (bf16[1,16,16,2,256]{4,1,0,3,2:T(8,128)(2,1)}, bf16[1,16,16,2,256]{4,1,0,3,2:T(8,128)(2,1)}, u32[]{:S(2)}, u32[]{:S(2)}) collective-permute-start(bf16[1,16,16,2,256]{4,1,0,3,2:T(8,128)(2,1)} %get-tuple-element.17), channel_id=1, source_target_pairs={{0,7},{1,6},{2,5},{3,4},{4,3},{5,2},{6,1},{7,0},{8,15},{9,14},{10,... | collective-permute-start | bytes 786440 | tf_op jit(solution)/shard_map/ppermute | solution.py:64
  258.0 20.8 %copy-start.4 = (bf16[1,16,16,2,256]{4,1,0,3,2:T(8,128)(2,1)}, bf16[1,16,16,2,256]{4,1,0,3,2:T(8,128)(2,1)S(1)}, u32[]{:S(2)}) copy-start(bf16[1,16,16,2,256]{4,1,0,3,2:T(8,128)(2,1)S(1)} %collective-permute-done.3) | copy-start | bytes 786436
  258.0 60.4 %collective-permute-start.6 = (bf16[1,16,16,2,256]{4,1,0,3,2:T(8,128)(2,1)}, bf16[1,16,16,2,256]{4,1,0,3,2:T(8,128)(2,1)}, u32[]{:S(2)}, u32[]{:S(2)}) collective-permute-start(bf16[1,16,16,2,256]{4,1,0,3,2:T(8,128)(2,1)} %get-tuple-element.18), channel_id=1, source_target_pairs={{0,6},{1,7},{2,4},{3,5},{4,2},{5,3},{6,0},{7,1},{8,14},{9,15},{10,... | collective-permute-start | bytes 786440 | tf_op jit(solution)/shard_map/ppermute | solution.py:64
  274.9 3.9 copy-start.5
  274.9 37.3 %collective-permute-start.5 = (bf16[1,16,16,2,256]{4,1,0,3,2:T(8,128)(2,1)}, bf16[1,16,16,2,256]{4,1,0,3,2:T(8,128)(2,1)}, u32[]{:S(2)}, u32[]{:S(2)}) collective-permute-start(bf16[1,16,16,2,256]{4,1,0,3,2:T(8,128)(2,1)} %get-tuple-element.19), channel_id=1, source_target_pairs={{0,5},{1,4},{2,7},{3,6},{4,1},{5,0},{6,3},{7,2},{8,13},{9,12},{10,... | collective-permute-start | bytes 786440 | tf_op jit(solution)/shard_map/ppermute | solution.py:64
  277.1 1.7 copy-start.7
  277.1 27.9 %collective-permute-start.4 = (bf16[1,16,16,2,256]{4,1,0,3,2:T(8,128)(2,1)}, bf16[1,16,16,2,256]{4,1,0,3,2:T(8,128)(2,1)}, u32[]{:S(2)}, u32[]{:S(2)}) collective-permute-start(bf16[1,16,16,2,256]{4,1,0,3,2:T(8,128)(2,1)} %get-tuple-element.20), channel_id=1, source_target_pairs={{0,4},{1,5},{2,6},{3,7},{4,0},{5,1},{6,2},{7,3},{8,12},{9,13},{10,... | collective-permute-start | bytes 786440 | tf_op jit(solution)/shard_map/ppermute | solution.py:64
  280.8 17.3 %copy-start.6 = (bf16[1,16,16,2,256]{4,1,0,3,2:T(8,128)(2,1)S(1)}, bf16[1,16,16,2,256]{4,1,0,3,2:T(8,128)(2,1)}, u32[]{:S(2)}) copy-start(bf16[1,16,16,2,256]{4,1,0,3,2:T(8,128)(2,1)} %copy-done.5) | copy-start | bytes 786436
  301.3 79.7 %copy-start.3 = (bf16[1,16,16,2,256]{4,1,0,3,2:T(8,128)(2,1)S(1)}, bf16[1,16,16,2,256]{4,1,0,3,2:T(8,128)(2,1)}, u32[]{:S(2)}) copy-start(bf16[1,16,16,2,256]{4,1,0,3,2:T(8,128)(2,1)} %get-tuple-element.13) | copy-start | bytes 786436
  305.0 128.5 %collective-permute-start.15 = (bf16[1,16,16,2,256]{4,1,0,3,2:T(8,128)(2,1)S(1)}, bf16[1,16,16,2,256]{4,1,0,3,2:T(8,128)(2,1)}, u32[]{:S(2)}, u32[]{:S(2)}) collective-permute-start(bf16[1,16,16,2,256]{4,1,0,3,2:T(8,128)(2,1)S(1)} %get-tuple-element.9), channel_id=1, source_target_pairs={{0,15},{1,14},{2,13},{3,12},{4,11},{5,10},{6,9},{7,8},{8,7},{9,6},... | collective-permute-start | bytes 786440 | tf_op jit(solution)/shard_map/ppermute | solution.py:64
  312.2 112.6 %collective-permute-start.14 = (bf16[1,16,16,2,256]{4,1,0,3,2:T(8,128)(2,1)S(1)}, bf16[1,16,16,2,256]{4,1,0,3,2:T(8,128)(2,1)}, u32[]{:S(2)}, u32[]{:S(2)}) collective-permute-start(bf16[1,16,16,2,256]{4,1,0,3,2:T(8,128)(2,1)S(1)} %get-tuple-element.10), channel_id=1, source_target_pairs={{0,14},{1,15},{2,12},{3,13},{4,10},{5,11},{6,8},{7,9},{8,6},{9,7},... | collective-permute-start | bytes 786440 | tf_op jit(solution)/shard_map/ppermute | solution.py:64
  318.4 97.1 %collective-permute-start.13 = (bf16[1,16,16,2,256]{4,1,0,3,2:T(8,128)(2,1)S(1)}, bf16[1,16,16,2,256]{4,1,0,3,2:T(8,128)(2,1)}, u32[]{:S(2)}, u32[]{:S(2)}) collective-permute-start(bf16[1,16,16,2,256]{4,1,0,3,2:T(8,128)(2,1)S(1)} %get-tuple-element.11), channel_id=1, source_target_pairs={{0,13},{1,12},{2,15},{3,14},{4,9},{5,8},{6,11},{7,10},{8,5},{9,4},... | collective-permute-start | bytes 786440 | tf_op jit(solution)/shard_map/ppermute | solution.py:64
  326.3 78.1 %collective-permute-start.12 = (bf16[1,16,16,2,256]{4,1,0,3,2:T(8,128)(2,1)S(1)}, bf16[1,16,16,2,256]{4,1,0,3,2:T(8,128)(2,1)}, u32[]{:S(2)}, u32[]{:S(2)}) collective-permute-start(bf16[1,16,16,2,256]{4,1,0,3,2:T(8,128)(2,1)S(1)} %get-tuple-element.12), channel_id=1, source_target_pairs={{0,12},{1,13},{2,14},{3,15},{4,8},{5,9},{6,10},{7,11},{8,4},{9,5},... | collective-permute-start | bytes 786440 | tf_op jit(solution)/shard_map/ppermute | solution.py:64
  331.1 33.9 %collective-permute-start.9 = (bf16[1,16,16,2,256]{4,1,0,3,2:T(8,128)(2,1)}, bf16[1,16,16,2,256]{4,1,0,3,2:T(8,128)(2,1)}, u32[]{:S(2)}, u32[]{:S(2)}) collective-permute-start(bf16[1,16,16,2,256]{4,1,0,3,2:T(8,128)(2,1)} %get-tuple-element.15), channel_id=1, source_target_pairs={{0,9},{1,8},{2,11},{3,10},{4,13},{5,12},{6,15},{7,14},{8,1},{9,0},... | collective-permute-start | bytes 786440 | tf_op jit(solution)/shard_map/ppermute | solution.py:64
  365.0 15.9 %collective-permute-start.10 = (bf16[1,16,16,2,256]{4,1,0,3,2:T(8,128)(2,1)}, bf16[1,16,16,2,256]{4,1,0,3,2:T(8,128)(2,1)}, u32[]{:S(2)}, u32[]{:S(2)}) collective-permute-start(bf16[1,16,16,2,256]{4,1,0,3,2:T(8,128)(2,1)} %get-tuple-element.14), channel_id=1, source_target_pairs={{0,10},{1,11},{2,8},{3,9},{4,14},{5,15},{6,12},{7,13},{8,2},{9,3},... | collective-permute-start | bytes 786440 | tf_op jit(solution)/shard_map/ppermute | solution.py:64
  372.0 27.3 %copy-start.1 = (bf16[1,16,16,2,256]{2,1,4,3,0:T(8,128)(2,1)S(1)}, bf16[1,16,16,2,256]{2,1,4,3,0:T(8,128)(2,1)}, u32[]{:S(2)}) copy-start(bf16[1,16,16,2,256]{2,1,4,3,0:T(8,128)(2,1)} %copy.15) | copy-start | bytes 786436
  381.0 13.6 %collective-permute-start.11 = (bf16[1,16,16,2,256]{4,1,0,3,2:T(8,128)(2,1)S(1)}, bf16[1,16,16,2,256]{4,1,0,3,2:T(8,128)(2,1)}, u32[]{:S(2)}, u32[]{:S(2)}) collective-permute-start(bf16[1,16,16,2,256]{4,1,0,3,2:T(8,128)(2,1)S(1)} %copy-done.3), channel_id=1, source_target_pairs={{0,11},{1,10},{2,9},{3,8},{4,15},{5,14},{6,13},{7,12},{8,3},{9,2},... | collective-permute-start | bytes 786440 | tf_op jit(solution)/shard_map/ppermute | solution.py:64
  401.0 19.0 %copy-start.2 = (bf16[1,16,16,2,256]{2,1,4,3,0:T(8,128)(2,1)S(1)}, bf16[1,16,16,2,256]{2,1,4,3,0:T(8,128)(2,1)}, u32[]{:S(2)}) copy-start(bf16[1,16,16,2,256]{2,1,4,3,0:T(8,128)(2,1)} %copy.19) | copy-start | bytes 786436
  639.0 62.9 %copy-start = (pred[1024,1024]{1,0:T(8,128)(4,1)S(1)}, pred[1024,1024]{1,0:T(8,128)(4,1)}, u32[]{:S(2)}) copy-start(pred[1024,1024]{1,0:T(8,128)(4,1)} %iota_compare_fusion) | copy-start | bytes 3145732
